TPU v7x, 32 devices: a whole 2x2x4 slice. The times are simulated.
32 devices in a mesh: site: 4 (over y, x), bond: 8 (over z, core).
Axes of the slice: x: 2, y: 2, z: 4, core: 2. Of those that a mesh axis runs over, the one named last changes fastest.
Arguments:
- start_rows: bfloat16 [1024, 4096], P(None, 'bond'), may hold values from -6 to 6
- site_tensors: bfloat16 [4, 4096, 8, 4096], P('site', None, None, 'bond'), may hold values from -0.09375 to 0.09375
- block_scales: float32 [4, 8, 32], P('site', None, 'bond'), may hold values from 0.25 to 1
- displacement: float32 [4, 8, 8], P('site'), may hold values from -0.9 to 0.9
- outcomes: int32 [4, 1024], P('site'), may hold values from 0 to 7
Outputs:
- leaving: bfloat16 [4, 1024, 4096], P('site', None, 'bond')
- log_norms: float32 [4, 1024], P('site')
Inputs may be any that keep to these rules, and one draw needn't show every extreme that they name: outcomes index the second dimension of displacement.
All inputs are finite; a program needn't handle non-finite values.
Results may differ from a plain program's by a relative error of at most 0.014.
Values may be sent and summed in bfloat16 or wider, within the bound.
A program may use at most 128 MiB of HBM per device.

v0:
```python
import jax
import jax.numpy as jnp
from jax import lax
from jax.sharding import PartitionSpec as P

ROWS = 512


def shifted(value, axis, steps):
    count = lax.axis_size(axis)
    initial, last = (max(0, -steps), min(count, count - steps))
    return lax.ppermute(value, axis, [(source, source + steps) for source in range(initial, last)])


def local(start_rows, site_tensors, block_scales, displacement, outcomes):
    sites = lax.axis_size("site")
    cols = site_tensors.shape[3]
    chi = site_tensors.shape[1]
    phys = site_tensors.shape[2]
    nblk = block_scales.shape[2]
    allrows = start_rows.shape[0]
    grows = ROWS
    ngroups = allrows // grows
    ticks = ngroups + sites - 1
    a_mat = site_tensors[0].reshape(chi, phys * cols)
    scales = block_scales[0][:, :, None]
    table = displacement[0]
    outcome_row = outcomes[0]
    position = lax.axis_index("site")

    def tick(step, carry):
        incoming, incoming_norm, out_leave, out_logs = carry
        batch = step - position
        valid = jnp.logical_and(batch >= 0, batch < ngroups)
        first = jnp.clip(batch, 0, ngroups - 1) * grows
        start_piece = lax.dynamic_slice_in_dim(start_rows, first, grows, 0)
        rows_in = jnp.where(position == 0, start_piece, incoming)
        piece = lax.all_gather(rows_in, "bond", axis=1, tiled=True)
        total = jnp.dot(piece, a_mat, preferred_element_type=jnp.float32)
        pf = piece.astype(jnp.float32)
        total, squares = (total, jnp.sum(pf * pf, axis=1))
        local_norm = jnp.sqrt(squares / chi + 1e-06)
        prod = total.reshape(grows, phys, nblk, cols // nblk) * scales[None]
        prod = prod.reshape(grows, phys, cols)
        picked = lax.dynamic_slice_in_dim(outcome_row, first, grows, 0)
        onehot = (picked[:, None] == jnp.arange(phys, dtype=jnp.int32)[None, :]).astype(jnp.float32)
        weight = jnp.dot(onehot, table, precision=lax.Precision.HIGHEST)
        mixed = jnp.sum(weight[:, :, None] * prod, axis=1)
        leave = (mixed / local_norm[:, None]).astype(jnp.bfloat16)
        out_leave = jnp.where(
            valid, lax.dynamic_update_slice_in_dim(out_leave, leave, first, 0), out_leave
        )
        out_logs = jnp.where(
            valid,
            lax.dynamic_update_slice_in_dim(out_logs, jnp.log(local_norm), first, 0),
            out_logs,
        )
        incoming = shifted(leave, "site", 1)
        return (incoming, incoming_norm, out_leave, out_logs)

    carry = (
        jnp.zeros((grows, cols), jnp.bfloat16),
        jnp.ones((grows,), jnp.float32),
        jnp.zeros((allrows, cols), jnp.bfloat16),
        jnp.zeros((allrows,), jnp.float32),
    )
    carry = lax.fori_loop(0, ticks, tick, carry)
    return (carry[2][None], carry[3][None])


def solution(mesh):
    return jax.shard_map(
        local,
        mesh=mesh,
        in_specs=(
            P(None, "bond"),
            P("site", None, None, "bond"),
            P("site", None, "bond"),
            P("site", None, None),
            P("site", None),
        ),
        out_specs=(P("site", None, "bond"), P("site", None)),
        check_vma=False,
    )
```

profile of v0, /device:TPU:4, one launch (start us, length us, event | category | flops | bytes accessed | tf_op | source)
XLA Modules:
  0.0 550.5 jit_solution(6089565585654436752)
XLA Ops:
  7.2 22.7 %copy.10 = bf16[512,8,8,512]{3,1,2,0:T(8,128)(2,1)} copy(bf16[512,8,8,512]{3,2,1,0:T(8,128)(2,1)} %bitcast.35) | data formatting | bytes 67108864
  31.1 512.3 %while.18 = (s32[]{:T(128)}, bf16[512,512]{1,0:T(8,128)(2,1)S(1)}, bf16[1024,512]{1,0:T(8,128)(2,1)}, f32[1024]{0:T(1024)S(1)}, s32[]{:T(128)}, /*index=5*/s32[1...) while((s32[]{:T(128)}, bf16[512,512]{1,0:T(8,128)(2,1)S(1)}, ...), condition=%wide.region_3.4_spmd, body=%wide.region_0.3_spmd.sunk | while | flops 17193637888 | bytes 113855224 | solution.py:67
  33.6 47.9 %all-gather.2.cloned.1.call-done = bf16[512,4096]{1,0:T(8,128)(2,1)} async-done(((bf16[512,512]{1,0:T(8,128)(2,1)}), bf16[512,4096]{1,0:T(8,128)(2,1)}) %all-gather.2.cloned.1.call-update) | async-done | bytes 4194320 | tf_op jit(solution)/shard_map/while/body/eval_jaxpr/all_gather | solution.py:38
  81.6 22.6 %fusion.18 = f32[512,4096]{1,0:T(8,128)S(1)} fusion(bf16[512,4096]{1,0:T(8,128)(2,1)} %all-gather.2.cloned.1.call-done, bf16[4096,4096]{1,0:T(8,128)(2,1)} %get-tuple-element.361), kind=kOutput, calls=%fused_computation.14.clone.1 | convolution fusion | flops 17179869184 | bytes 46137344 | tf_op jit(solution)/shard_map/while/body/eval_jaxpr/dot_general | solution.py:39
  104.2 8.2 %copy.12 = f32[64,8,8,512]{3,2,1,0:T(8,128)S(1)} copy(f32[64,8,8,512]{3,1,2,0:T(8,128)S(1)} %bitcast.34) | data formatting | bytes 16777216 | tf_op jit(solution)/shard_map/while
  113.5 3.9 fusion.20
  119.4 3.4 collective-permute-start
  122.8 13.5 %collective-permute-done = bf16[512,512]{1,0:T(8,128)(2,1)S(1)} collective-permute-done((bf16[512,512]{1,0:T(8,128)(2,1)S(1)}, bf16[512,512]{1,0:T(8,128)(2,1)S(1)}, u32[]{:S(2)}, u32[]{:S(2)}) %collective-permute-start) | collective-permute-done | bytes 524320 | tf_op jit(solution)/shard_map/while/body/eval_jaxpr/ppermute | solution.py:12
  138.8 44.7 %all-gather.2.cloned.1.call-done = bf16[512,4096]{1,0:T(8,128)(2,1)} async-done(((bf16[512,512]{1,0:T(8,128)(2,1)}), bf16[512,4096]{1,0:T(8,128)(2,1)}) %all-gather.2.cloned.1.call-update) | async-done | bytes 4194320 | tf_op jit(solution)/shard_map/while/body/eval_jaxpr/all_gather | solution.py:38
  183.5 22.6 %fusion.18 = f32[512,4096]{1,0:T(8,128)S(1)} fusion(bf16[512,4096]{1,0:T(8,128)(2,1)} %all-gather.2.cloned.1.call-done, bf16[4096,4096]{1,0:T(8,128)(2,1)} %get-tuple-element.361), kind=kOutput, calls=%fused_computation.14.clone.1 | convolution fusion | flops 17179869184 | bytes 46137344 | tf_op jit(solution)/shard_map/while/body/eval_jaxpr/dot_general | solution.py:39
  206.1 8.2 %copy.12 = f32[64,8,8,512]{3,2,1,0:T(8,128)S(1)} copy(f32[64,8,8,512]{3,1,2,0:T(8,128)S(1)} %bitcast.34) | data formatting | bytes 16777216 | tf_op jit(solution)/shard_map/while
  215.4 3.9 fusion.20
  221.4 3.4 collective-permute-start
  224.7 13.5 %collective-permute-done = bf16[512,512]{1,0:T(8,128)(2,1)S(1)} collective-permute-done((bf16[512,512]{1,0:T(8,128)(2,1)S(1)}, bf16[512,512]{1,0:T(8,128)(2,1)S(1)}, u32[]{:S(2)}, u32[]{:S(2)}) %collective-permute-start) | collective-permute-done | bytes 524320 | tf_op jit(solution)/shard_map/while/body/eval_jaxpr/ppermute | solution.py:12
  240.7 44.7 %all-gather.2.cloned.1.call-done = bf16[512,4096]{1,0:T(8,128)(2,1)} async-done(((bf16[512,512]{1,0:T(8,128)(2,1)}), bf16[512,4096]{1,0:T(8,128)(2,1)}) %all-gather.2.cloned.1.call-update) | async-done | bytes 4194320 | tf_op jit(solution)/shard_map/while/body/eval_jaxpr/all_gather | solution.py:38
  285.4 22.6 %fusion.18 = f32[512,4096]{1,0:T(8,128)S(1)} fusion(bf16[512,4096]{1,0:T(8,128)(2,1)} %all-gather.2.cloned.1.call-done, bf16[4096,4096]{1,0:T(8,128)(2,1)} %get-tuple-element.361), kind=kOutput, calls=%fused_computation.14.clone.1 | convolution fusion | flops 17179869184 | bytes 46137344 | tf_op jit(solution)/shard_map/while/body/eval_jaxpr/dot_general | solution.py:39
  308.0 8.2 %copy.12 = f32[64,8,8,512]{3,2,1,0:T(8,128)S(1)} copy(f32[64,8,8,512]{3,1,2,0:T(8,128)S(1)} %bitcast.34) | data formatting | bytes 16777216 | tf_op jit(solution)/shard_map/while
  317.3 3.9 fusion.20
  323.3 3.4 collective-permute-start
  326.6 13.5 %collective-permute-done = bf16[512,512]{1,0:T(8,128)(2,1)S(1)} collective-permute-done((bf16[512,512]{1,0:T(8,128)(2,1)S(1)}, bf16[512,512]{1,0:T(8,128)(2,1)S(1)}, u32[]{:S(2)}, u32[]{:S(2)}) %collective-permute-start) | collective-permute-done | bytes 524320 | tf_op jit(solution)/shard_map/while/body/eval_jaxpr/ppermute | solution.py:12
  342.6 44.4 %all-gather.2.cloned.1.call-done = bf16[512,4096]{1,0:T(8,128)(2,1)} async-done(((bf16[512,512]{1,0:T(8,128)(2,1)}), bf16[512,4096]{1,0:T(8,128)(2,1)}) %all-gather.2.cloned.1.call-update) | async-done | bytes 4194320 | tf_op jit(solution)/shard_map/while/body/eval_jaxpr/all_gather | solution.py:38
  387.0 22.6 %fusion.18 = f32[512,4096]{1,0:T(8,128)S(1)} fusion(bf16[512,4096]{1,0:T(8,128)(2,1)} %all-gather.2.cloned.1.call-done, bf16[4096,4096]{1,0:T(8,128)(2,1)} %get-tuple-element.361), kind=kOutput, calls=%fused_computation.14.clone.1 | convolution fusion | flops 17179869184 | bytes 46137344 | tf_op jit(solution)/shard_map/while/body/eval_jaxpr/dot_general | solution.py:39
  409.7 8.2 %copy.12 = f32[64,8,8,512]{3,2,1,0:T(8,128)S(1)} copy(f32[64,8,8,512]{3,1,2,0:T(8,128)S(1)} %bitcast.34) | data formatting | bytes 16777216 | tf_op jit(solution)/shard_map/while
  418.9 3.9 fusion.20
  424.9 3.4 collective-permute-start
  428.3 13.5 %collective-permute-done = bf16[512,512]{1,0:T(8,128)(2,1)S(1)} collective-permute-done((bf16[512,512]{1,0:T(8,128)(2,1)S(1)}, bf16[512,512]{1,0:T(8,128)(2,1)S(1)}, u32[]{:S(2)}, u32[]{:S(2)}) %collective-permute-start) | collective-permute-done | bytes 524320 | tf_op jit(solution)/shard_map/while/body/eval_jaxpr/ppermute | solution.py:12
  444.2 44.4 %all-gather.2.cloned.1.call-done = bf16[512,4096]{1,0:T(8,128)(2,1)} async-done(((bf16[512,512]{1,0:T(8,128)(2,1)}), bf16[512,4096]{1,0:T(8,128)(2,1)}) %all-gather.2.cloned.1.call-update) | async-done | bytes 4194320 | tf_op jit(solution)/shard_map/while/body/eval_jaxpr/all_gather | solution.py:38
  488.7 22.6 %fusion.18 = f32[512,4096]{1,0:T(8,128)S(1)} fusion(bf16[512,4096]{1,0:T(8,128)(2,1)} %all-gather.2.cloned.1.call-done, bf16[4096,4096]{1,0:T(8,128)(2,1)} %get-tuple-element.361), kind=kOutput, calls=%fused_computation.14.clone.1 | convolution fusion | flops 17179869184 | bytes 46137344 | tf_op jit(solution)/shard_map/while/body/eval_jaxpr/dot_general | solution.py:39
  511.3 8.2 %copy.12 = f32[64,8,8,512]{3,2,1,0:T(8,128)S(1)} copy(f32[64,8,8,512]{3,1,2,0:T(8,128)S(1)} %bitcast.34) | data formatting | bytes 16777216 | tf_op jit(solution)/shard_map/while
  520.6 3.9 fusion.20
  526.5 3.4 collective-permute-start
  529.9 13.5 %collective-permute-done = bf16[512,512]{1,0:T(8,128)(2,1)S(1)} collective-permute-done((bf16[512,512]{1,0:T(8,128)(2,1)S(1)}, bf16[512,512]{1,0:T(8,128)(2,1)S(1)}, u32[]{:S(2)}, u32[]{:S(2)}) %collective-permute-start) | collective-permute-done | bytes 524320 | tf_op jit(solution)/shard_map/while/body/eval_jaxpr/ppermute | solution.py:12
  (66 shorter events, 29.9 us)
Async XLA Ops:
  7.2 23.9 %copy-start.1 = (f32[1,8,8]{2,1,0:T(8,128)S(1)}, f32[1,8,8]{2,1,0:T(8,128)}, u32[]{:S(2)}) copy-start(f32[1,8,8]{2,1,0:T(8,128)} %param.10) | copy-start | bytes 772
  7.2 23.9 %copy-start.2 = (f32[1,8,4]{1,2,0:T(4,128)S(1)}, f32[1,8,4]{1,2,0:T(4,128)}, u32[]{:S(2)}) copy-start(f32[1,8,4]{1,2,0:T(4,128)} %param.9) | copy-start | bytes 388
  7.2 23.9 %copy-start.4 = (s32[1,1024]{1,0:T(1,128)S(1)}, s32[1,1024]{1,0:T(1,128)}, u32[]{:S(2)}) copy-start(s32[1,1024]{1,0:T(1,128)} %param.11) | copy-start | bytes 12292
  31.1 50.5 %all-gather.2.cloned.1.call-start = ((), (), s32[]{:S(2)}) async-start(), calls=%async_computation | async-start | bytes 4718592 | tf_op jit(solution)/shard_map/while/body/eval_jaxpr/all_gather | solution.py:38
  104.2 8.2 %copy-start = (bf16[512,4096]{1,0:T(8,128)(2,1)S(1)}, bf16[512,4096]{1,0:T(8,128)(2,1)}, u32[]{:S(2)}) copy-start(bf16[512,4096]{1,0:T(8,128)(2,1)} %all-gather.2.cloned.1.call-done) | copy-start | bytes 12582916 | tf_op jit(solution)/shard_map/while
  119.4 16.8 %collective-permute-start = (bf16[512,512]{1,0:T(8,128)(2,1)S(1)}, bf16[512,512]{1,0:T(8,128)(2,1)S(1)}, u32[]{:S(2)}, u32[]{:S(2)}) collective-permute-start(bf16[512,512]{1,0:T(8,128)(2,1)S(1)} %get-tuple-element.317), channel_id=1, source_target_pairs={{0,8},{8,16},{16,24},{1,9},{9,17},{17,25},{2,10},{10,18},{18,26},{... | collective-permute-start | bytes 1572872 | tf_op jit(solution)/shard_map/while/body/eval_jaxpr/ppermute | solution.py:12
  136.3 47.2 %all-gather.2.cloned.1.call-start = ((), (), s32[]{:S(2)}) async-start(), calls=%async_computation | async-start | bytes 4718592 | tf_op jit(solution)/shard_map/while/body/eval_jaxpr/all_gather | solution.py:38
  206.1 8.2 %copy-start = (bf16[512,4096]{1,0:T(8,128)(2,1)S(1)}, bf16[512,4096]{1,0:T(8,128)(2,1)}, u32[]{:S(2)}) copy-start(bf16[512,4096]{1,0:T(8,128)(2,1)} %all-gather.2.cloned.1.call-done) | copy-start | bytes 12582916 | tf_op jit(solution)/shard_map/while
  221.4 16.8 %collective-permute-start = (bf16[512,512]{1,0:T(8,128)(2,1)S(1)}, bf16[512,512]{1,0:T(8,128)(2,1)S(1)}, u32[]{:S(2)}, u32[]{:S(2)}) collective-permute-start(bf16[512,512]{1,0:T(8,128)(2,1)S(1)} %get-tuple-element.317), channel_id=1, source_target_pairs={{0,8},{8,16},{16,24},{1,9},{9,17},{17,25},{2,10},{10,18},{18,26},{... | collective-permute-start | bytes 1572872 | tf_op jit(solution)/shard_map/while/body/eval_jaxpr/ppermute | solution.py:12
  238.2 47.2 %all-gather.2.cloned.1.call-start = ((), (), s32[]{:S(2)}) async-start(), calls=%async_computation | async-start | bytes 4718592 | tf_op jit(solution)/shard_map/while/body/eval_jaxpr/all_gather | solution.py:38
  308.0 8.2 %copy-start = (bf16[512,4096]{1,0:T(8,128)(2,1)S(1)}, bf16[512,4096]{1,0:T(8,128)(2,1)}, u32[]{:S(2)}) copy-start(bf16[512,4096]{1,0:T(8,128)(2,1)} %all-gather.2.cloned.1.call-done) | copy-start | bytes 12582916 | tf_op jit(solution)/shard_map/while
  323.3 16.8 %collective-permute-start = (bf16[512,512]{1,0:T(8,128)(2,1)S(1)}, bf16[512,512]{1,0:T(8,128)(2,1)S(1)}, u32[]{:S(2)}, u32[]{:S(2)}) collective-permute-start(bf16[512,512]{1,0:T(8,128)(2,1)S(1)} %get-tuple-element.317), channel_id=1, source_target_pairs={{0,8},{8,16},{16,24},{1,9},{9,17},{17,25},{2,10},{10,18},{18,26},{... | collective-permute-start | bytes 1572872 | tf_op jit(solution)/shard_map/while/body/eval_jaxpr/ppermute | solution.py:12
  340.1 46.9 %all-gather.2.cloned.1.call-start = ((), (), s32[]{:S(2)}) async-start(), calls=%async_computation | async-start | bytes 4718592 | tf_op jit(solution)/shard_map/while/body/eval_jaxpr/all_gather | solution.py:38
  409.6 8.2 %copy-start = (bf16[512,4096]{1,0:T(8,128)(2,1)S(1)}, bf16[512,4096]{1,0:T(8,128)(2,1)}, u32[]{:S(2)}) copy-start(bf16[512,4096]{1,0:T(8,128)(2,1)} %all-gather.2.cloned.1.call-done) | copy-start | bytes 12582916 | tf_op jit(solution)/shard_map/while
  424.9 16.8 %collective-permute-start = (bf16[512,512]{1,0:T(8,128)(2,1)S(1)}, bf16[512,512]{1,0:T(8,128)(2,1)S(1)}, u32[]{:S(2)}, u32[]{:S(2)}) collective-permute-start(bf16[512,512]{1,0:T(8,128)(2,1)S(1)} %get-tuple-element.317), channel_id=1, source_target_pairs={{0,8},{8,16},{16,24},{1,9},{9,17},{17,25},{2,10},{10,18},{18,26},{... | collective-permute-start | bytes 1572872 | tf_op jit(solution)/shard_map/while/body/eval_jaxpr/ppermute | solution.py:12
  441.7 46.9 %all-gather.2.cloned.1.call-start = ((), (), s32[]{:S(2)}) async-start(), calls=%async_computation | async-start | bytes 4718592 | tf_op jit(solution)/shard_map/while/body/eval_jaxpr/all_gather | solution.py:38
  511.3 8.2 %copy-start = (bf16[512,4096]{1,0:T(8,128)(2,1)S(1)}, bf16[512,4096]{1,0:T(8,128)(2,1)}, u32[]{:S(2)}) copy-start(bf16[512,4096]{1,0:T(8,128)(2,1)} %all-gather.2.cloned.1.call-done) | copy-start | bytes 12582916 | tf_op jit(solution)/shard_map/while
  526.5 16.8 %collective-permute-start = (bf16[512,512]{1,0:T(8,128)(2,1)S(1)}, bf16[512,512]{1,0:T(8,128)(2,1)S(1)}, u32[]{:S(2)}, u32[]{:S(2)}) collective-permute-start(bf16[512,512]{1,0:T(8,128)(2,1)S(1)} %get-tuple-element.317), channel_id=1, source_target_pairs={{0,8},{8,16},{16,24},{1,9},{9,17},{17,25},{2,10},{10,18},{18,26},{... | collective-permute-start | bytes 1572872 | tf_op jit(solution)/shard_map/while/body/eval_jaxpr/ppermute | solution.py:12
  543.4 0.6 copy-start.3
Sparse Core Ops, SparseCore 0:
  33.5 48.0 all-gather.1
  138.7 44.7 all-gather.1
  240.6 44.7 all-gather.1
  342.2 44.7 all-gather.1
  443.9 44.7 all-gather.1
where the time goes:
time: 551 us
  waiting for transfers between devices  294 us (53%)
  matrix products  115 us (21%)
  local copies, waits for them, and re-layouts  66 us (12%)
  other arithmetic  45.2 us (8%)
  starting transfers between devices  16.9 us (3%)
  between operations  13.8 us (3%)
    all_gather x5, waiting for transfers between devices, tick(): piece = lax.all_gather(rows_in, 'bond', axis=1, tiled=True)  226 us
    dot_general x5, matrix products, tick(): total = jnp.dot(piece, a_mat, preferred_element_type=jnp.float32)  113 us
    ppermute x5, waiting for transfers between devices, shifted(): lax.ppermute(value, axis, [(source, source + steps) for source in range(i...  67.3 us
    while x15, local copies, waits for them, and re-layouts  40.9 us
    unnamed x9, local copies, waits for them, and re-layouts  23.3 us
    reduce_sum x5, other arithmetic, tick(): mixed = jnp.sum(weight[:, :, None] * prod, axis=1)  19.5 us
    ppermute x5, starting transfers between devices, shifted(): lax.ppermute(value, axis, [(source, source + steps) for source in range(i...  16.8 us
  transfers between devices with their start and end apart: 10, of which 10 were waited for; matrix products, arithmetic and copies ran while one was open for 0% of the time, Pallas kernels for 0%

commit v1 on v0

--- a/solution.py
+++ b/solution.py
@@ -35,7 +35,16 @@
         first = jnp.clip(batch, 0, ngroups - 1) * grows
         start_piece = lax.dynamic_slice_in_dim(start_rows, first, grows, 0)
         rows_in = jnp.where(position == 0, start_piece, incoming)
-        piece = lax.all_gather(rows_in, "bond", axis=1, tiled=True)
+        wide_out, long_array = (jax.lax.axis_size("bond"), jax.lax.axis_index("bond"))
+        piece, mat_out = (rows_in, 1)
+        while mat_out < wide_out:
+            s_next = jax.lax.ppermute(
+                piece, axis_name="bond", perm=[(nth, nth ^ mat_out) for nth in range(wide_out)]
+            )
+            p_next = jnp.concatenate([piece, s_next], 1)
+            piece_out = jnp.concatenate([s_next, piece], 1)
+            piece = jnp.where(long_array & mat_out == 0, p_next, piece_out)
+            mat_out = 2 * mat_out
         total = jnp.dot(piece, a_mat, preferred_element_type=jnp.float32)
         pf = piece.astype(jnp.float32)
         total, squares = (total, jnp.sum(pf * pf, axis=1))

time: 551 us -> 943 us (1.71)
  waiting for transfers between devices: 294 us -> 645 us
  other arithmetic: 45.2 us -> 68.1 us
  starting transfers between devices: 16.9 us -> 36 us
  between operations: 13.8 us -> 0.67 us
  matrix products: 115 us -> 126 us
    ppermute x0 -> x15, waiting for transfers between devices: none -> 578 us  [tick(): jax.lax.ppermute(piece, axis_name='bond', perm=[(nth, nth ^ mat_out) for...]
    all_gather x5 -> x0, waiting for transfers between devices: 226 us -> none  [tick(): piece = lax.all_gather(rows_in, 'bond', axis=1, tiled=True)]
    ppermute x0 -> x15, starting transfers between devices: none -> 24.4 us  [tick(): jax.lax.ppermute(piece, axis_name='bond', perm=[(nth, nth ^ mat_out) for...]
    reduce_sum x5, other arithmetic: 4.47 us -> 18.4 us  [tick(): total, squares = (total, jnp.sum(pf * pf, axis=1))]
    select_n x0 -> x10, other arithmetic: none -> 13.1 us  [tick(): piece = jnp.where(long_array & mat_out == 0, p_next, piece_out)]
    dot_general x5, matrix products: 113 us -> 124 us  [tick(): total = jnp.dot(piece, a_mat, preferred_element_type=jnp.float32)]
    while x15 -> x5, local copies, waits for them, and re-layouts: 40.9 us -> 40.5 us
  transfers between devices with their start and end apart: 10 -> 20, of which waited for: 10 -> 20; matrix products, arithmetic and copies ran while one was open for 0% -> 0% of each run, Pallas kernels for 0% -> 0%
where the time goes in v1:
time: 943 us; the launch traced here: 941 us
  waiting for transfers between devices  645 us (68%)
  matrix products  126 us (13%)
  other arithmetic  68.1 us (7%)
  local copies, waits for them, and re-layouts  65.7 us (7%)
  starting transfers between devices  36 us (4%)
    ppermute x15, waiting for transfers between devices, tick(): jax.lax.ppermute(piece, axis_name='bond', perm=[(nth, nth ^ mat_out) for...  578 us
    dot_general x5, matrix products, tick(): total = jnp.dot(piece, a_mat, preferred_element_type=jnp.float32)  124 us
    ppermute x5, waiting for transfers between devices, shifted(): lax.ppermute(value, axis, [(source, source + steps) for source in range(i...  66.9 us
    while x5, local copies, waits for them, and re-layouts  40.5 us
    ppermute x15, starting transfers between devices, tick(): jax.lax.ppermute(piece, axis_name='bond', perm=[(nth, nth ^ mat_out) for...  24.4 us
    unnamed x9, local copies, waits for them, and re-layouts  23.3 us
    reduce_sum x5, other arithmetic, tick(): mixed = jnp.sum(weight[:, :, None] * prod, axis=1)  19.5 us
  transfers between devices with their start and end apart: 20, of which 20 were waited for; matrix products, arithmetic and copies ran while one was open for 0% of the time, Pallas kernels for 0%

profile of v1, /device:TPU:4, one launch (start us, length us, event | category | flops | bytes accessed | tf_op | source)
XLA Modules:
  0.0 941.2 jit_solution(12995980864557633793)
XLA Ops:
  0.7 22.7 %copy.10 = bf16[512,8,8,512]{3,1,2,0:T(8,128)(2,1)} copy(bf16[512,8,8,512]{3,2,1,0:T(8,128)(2,1)} %bitcast.32) | data formatting | bytes 67108864
  24.5 916.1 %while.18 = (s32[]{:T(128)}, bf16[512,512]{1,0:T(8,128)(2,1)S(1)}, bf16[1024,512]{1,0:T(8,128)(2,1)}, f32[1024]{0:T(1024)S(1)}, s32[]{:T(128)}, /*index=5*/s32[1...) while((s32[]{:T(128)}, bf16[512,512]{1,0:T(8,128)(2,1)S(1)}, ...), condition=%wide.region_3.4_spmd, body=%wide.region_0.3_spmd.sunk | while | flops 17245542400 | bytes 103893904 | solution.py:76
  29.6 23.7 %collective-permute-done.1 = bf16[512,1024]{1,0:T(8,128)(2,1)} collective-permute-done((bf16[512,1024]{1,0:T(8,128)(2,1)S(1)}, bf16[512,1024]{1,0:T(8,128)(2,1)}, u32[]{:S(2)}, u32[]{:S(2)}) %collective-permute-start.1) | collective-permute-done | bytes 1048608 | tf_op jit(solution)/shard_map/while/body/eval_jaxpr/ppermute | solution.py:41
  58.8 89.7 %collective-permute-done.2 = bf16[512,2048]{1,0:T(8,128)(2,1)} collective-permute-done((bf16[512,2048]{1,0:T(8,128)(2,1)S(1)}, bf16[512,2048]{1,0:T(8,128)(2,1)}, u32[]{:S(2)}, u32[]{:S(2)}) %collective-permute-start.2) | collective-permute-done | bytes 2097184 | tf_op jit(solution)/shard_map/while/body/eval_jaxpr/ppermute | solution.py:41
  148.5 24.8 %fusion.16 = f32[512,4096]{1,0:T(8,128)S(1)} fusion(bf16[4096,4096]{1,0:T(8,128)(2,1)} %get-tuple-element.365, bf16[512,2048]{1,0:T(8,128)(2,1)} %collective-permute-done.2, bf16[512,2048]{1,0:T(8,128)(2,1)S(1)} %maximum_select_fusion.9, pred[]{:T(512)S(6)} %eq.86), kind=kOutput, calls=%fused_computation.8.clone.1 | convolution fusion | flops 17198743552 | bytes 46137344 | tf_op jit(solution)/shard_map/while/body/eval_jaxpr/dot_general | solution.py:48
  173.4 8.1 copy.12
  185.3 3.9 fusion.18
  194.7 12.2 %collective-permute-done.3 = bf16[512,512]{1,0:T(8,128)(2,1)S(1)} collective-permute-done((bf16[512,512]{1,0:T(8,128)(2,1)S(1)}, bf16[512,512]{1,0:T(8,128)(2,1)S(1)}, u32[]{:S(2)}, u32[]{:S(2)}) %collective-permute-start.3) | collective-permute-done | bytes 524320 | tf_op jit(solution)/shard_map/while/body/eval_jaxpr/ppermute | solution.py:12
  212.0 23.7 %collective-permute-done.1 = bf16[512,1024]{1,0:T(8,128)(2,1)} collective-permute-done((bf16[512,1024]{1,0:T(8,128)(2,1)S(1)}, bf16[512,1024]{1,0:T(8,128)(2,1)}, u32[]{:S(2)}, u32[]{:S(2)}) %collective-permute-start.1) | collective-permute-done | bytes 1048608 | tf_op jit(solution)/shard_map/while/body/eval_jaxpr/ppermute | solution.py:41
  242.0 89.9 %collective-permute-done.2 = bf16[512,2048]{1,0:T(8,128)(2,1)} collective-permute-done((bf16[512,2048]{1,0:T(8,128)(2,1)S(1)}, bf16[512,2048]{1,0:T(8,128)(2,1)}, u32[]{:S(2)}, u32[]{:S(2)}) %collective-permute-start.2) | collective-permute-done | bytes 2097184 | tf_op jit(solution)/shard_map/while/body/eval_jaxpr/ppermute | solution.py:41
  331.9 24.8 %fusion.16 = f32[512,4096]{1,0:T(8,128)S(1)} fusion(bf16[4096,4096]{1,0:T(8,128)(2,1)} %get-tuple-element.365, bf16[512,2048]{1,0:T(8,128)(2,1)} %collective-permute-done.2, bf16[512,2048]{1,0:T(8,128)(2,1)S(1)} %maximum_select_fusion.9, pred[]{:T(512)S(6)} %eq.86), kind=kOutput, calls=%fused_computation.8.clone.1 | convolution fusion | flops 17198743552 | bytes 46137344 | tf_op jit(solution)/shard_map/while/body/eval_jaxpr/dot_general | solution.py:48
  356.7 8.1 copy.12
  368.7 3.9 fusion.18
  377.2 13.2 %collective-permute-done.3 = bf16[512,512]{1,0:T(8,128)(2,1)S(1)} collective-permute-done((bf16[512,512]{1,0:T(8,128)(2,1)S(1)}, bf16[512,512]{1,0:T(8,128)(2,1)S(1)}, u32[]{:S(2)}, u32[]{:S(2)}) %collective-permute-start.3) | collective-permute-done | bytes 524320 | tf_op jit(solution)/shard_map/while/body/eval_jaxpr/ppermute | solution.py:12
  395.4 23.8 %collective-permute-done.1 = bf16[512,1024]{1,0:T(8,128)(2,1)} collective-permute-done((bf16[512,1024]{1,0:T(8,128)(2,1)S(1)}, bf16[512,1024]{1,0:T(8,128)(2,1)}, u32[]{:S(2)}, u32[]{:S(2)}) %collective-permute-start.1) | collective-permute-done | bytes 1048608 | tf_op jit(solution)/shard_map/while/body/eval_jaxpr/ppermute | solution.py:41
  425.4 89.9 %collective-permute-done.2 = bf16[512,2048]{1,0:T(8,128)(2,1)} collective-permute-done((bf16[512,2048]{1,0:T(8,128)(2,1)S(1)}, bf16[512,2048]{1,0:T(8,128)(2,1)}, u32[]{:S(2)}, u32[]{:S(2)}) %collective-permute-start.2) | collective-permute-done | bytes 2097184 | tf_op jit(solution)/shard_map/while/body/eval_jaxpr/ppermute | solution.py:41
  515.3 24.8 %fusion.16 = f32[512,4096]{1,0:T(8,128)S(1)} fusion(bf16[4096,4096]{1,0:T(8,128)(2,1)} %get-tuple-element.365, bf16[512,2048]{1,0:T(8,128)(2,1)} %collective-permute-done.2, bf16[512,2048]{1,0:T(8,128)(2,1)S(1)} %maximum_select_fusion.9, pred[]{:T(512)S(6)} %eq.86), kind=kOutput, calls=%fused_computation.8.clone.1 | convolution fusion | flops 17198743552 | bytes 46137344 | tf_op jit(solution)/shard_map/while/body/eval_jaxpr/dot_general | solution.py:48
  540.1 8.1 copy.12
  552.1 3.9 fusion.18
  560.0 13.8 %collective-permute-done.3 = bf16[512,512]{1,0:T(8,128)(2,1)S(1)} collective-permute-done((bf16[512,512]{1,0:T(8,128)(2,1)S(1)}, bf16[512,512]{1,0:T(8,128)(2,1)S(1)}, u32[]{:S(2)}, u32[]{:S(2)}) %collective-permute-start.3) | collective-permute-done | bytes 524320 | tf_op jit(solution)/shard_map/while/body/eval_jaxpr/ppermute | solution.py:12
  578.9 23.8 %collective-permute-done.1 = bf16[512,1024]{1,0:T(8,128)(2,1)} collective-permute-done((bf16[512,1024]{1,0:T(8,128)(2,1)S(1)}, bf16[512,1024]{1,0:T(8,128)(2,1)}, u32[]{:S(2)}, u32[]{:S(2)}) %collective-permute-start.1) | collective-permute-done | bytes 1048608 | tf_op jit(solution)/shard_map/while/body/eval_jaxpr/ppermute | solution.py:41
  608.8 89.9 %collective-permute-done.2 = bf16[512,2048]{1,0:T(8,128)(2,1)} collective-permute-done((bf16[512,2048]{1,0:T(8,128)(2,1)S(1)}, bf16[512,2048]{1,0:T(8,128)(2,1)}, u32[]{:S(2)}, u32[]{:S(2)}) %collective-permute-start.2) | collective-permute-done | bytes 2097184 | tf_op jit(solution)/shard_map/while/body/eval_jaxpr/ppermute | solution.py:41
  698.7 24.8 %fusion.16 = f32[512,4096]{1,0:T(8,128)S(1)} fusion(bf16[4096,4096]{1,0:T(8,128)(2,1)} %get-tuple-element.365, bf16[512,2048]{1,0:T(8,128)(2,1)} %collective-permute-done.2, bf16[512,2048]{1,0:T(8,128)(2,1)S(1)} %maximum_select_fusion.9, pred[]{:T(512)S(6)} %eq.86), kind=kOutput, calls=%fused_computation.8.clone.1 | convolution fusion | flops 17198743552 | bytes 46137344 | tf_op jit(solution)/shard_map/while/body/eval_jaxpr/dot_general | solution.py:48
  723.5 8.1 copy.12
  735.5 3.9 fusion.18
  743.4 13.8 %collective-permute-done.3 = bf16[512,512]{1,0:T(8,128)(2,1)S(1)} collective-permute-done((bf16[512,512]{1,0:T(8,128)(2,1)S(1)}, bf16[512,512]{1,0:T(8,128)(2,1)S(1)}, u32[]{:S(2)}, u32[]{:S(2)}) %collective-permute-start.3) | collective-permute-done | bytes 524320 | tf_op jit(solution)/shard_map/while/body/eval_jaxpr/ppermute | solution.py:12
  762.3 23.8 %collective-permute-done.1 = bf16[512,1024]{1,0:T(8,128)(2,1)} collective-permute-done((bf16[512,1024]{1,0:T(8,128)(2,1)S(1)}, bf16[512,1024]{1,0:T(8,128)(2,1)}, u32[]{:S(2)}, u32[]{:S(2)}) %collective-permute-start.1) | collective-permute-done | bytes 1048608 | tf_op jit(solution)/shard_map/while/body/eval_jaxpr/ppermute | solution.py:41
  792.2 89.9 %collective-permute-done.2 = bf16[512,2048]{1,0:T(8,128)(2,1)} collective-permute-done((bf16[512,2048]{1,0:T(8,128)(2,1)S(1)}, bf16[512,2048]{1,0:T(8,128)(2,1)}, u32[]{:S(2)}, u32[]{:S(2)}) %collective-permute-start.2) | collective-permute-done | bytes 2097184 | tf_op jit(solution)/shard_map/while/body/eval_jaxpr/ppermute | solution.py:41
  882.1 24.8 %fusion.16 = f32[512,4096]{1,0:T(8,128)S(1)} fusion(bf16[4096,4096]{1,0:T(8,128)(2,1)} %get-tuple-element.365, bf16[512,2048]{1,0:T(8,128)(2,1)} %collective-permute-done.2, bf16[512,2048]{1,0:T(8,128)(2,1)S(1)} %maximum_select_fusion.9, pred[]{:T(512)S(6)} %eq.86), kind=kOutput, calls=%fused_computation.8.clone.1 | convolution fusion | flops 17198743552 | bytes 46137344 | tf_op jit(solution)/shard_map/while/body/eval_jaxpr/dot_general | solution.py:48
  907.0 8.1 copy.12
  918.9 3.9 fusion.18
  926.8 13.8 %collective-permute-done.3 = bf16[512,512]{1,0:T(8,128)(2,1)S(1)} collective-permute-done((bf16[512,512]{1,0:T(8,128)(2,1)S(1)}, bf16[512,512]{1,0:T(8,128)(2,1)S(1)}, u32[]{:S(2)}, u32[]{:S(2)}) %collective-permute-start.3) | collective-permute-done | bytes 524320 | tf_op jit(solution)/shard_map/while/body/eval_jaxpr/ppermute | solution.py:12
  (81 shorter events, 98.1 us)
Async XLA Ops:
  0.6 23.9 %copy-start = (f32[1,8,8]{2,1,0:T(8,128)S(1)}, f32[1,8,8]{2,1,0:T(8,128)}, u32[]{:S(2)}) copy-start(f32[1,8,8]{2,1,0:T(8,128)} %param.10) | copy-start | bytes 772
  0.6 23.8 %copy-start.1 = (f32[1,8,4]{1,2,0:T(4,128)S(1)}, f32[1,8,4]{1,2,0:T(4,128)}, u32[]{:S(2)}) copy-start(f32[1,8,4]{1,2,0:T(4,128)} %param.9) | copy-start | bytes 388
  0.7 23.8 %copy-start.3 = (s32[1,1024]{1,0:T(1,128)S(1)}, s32[1,1024]{1,0:T(1,128)}, u32[]{:S(2)}) copy-start(s32[1,1024]{1,0:T(1,128)} %param.11) | copy-start | bytes 12292
  25.7 2.0 collective-permute-start
  28.0 25.4 %collective-permute-start.1 = (bf16[512,1024]{1,0:T(8,128)(2,1)S(1)}, bf16[512,1024]{1,0:T(8,128)(2,1)}, u32[]{:S(2)}, u32[]{:S(2)}) collective-permute-start(bf16[512,1024]{1,0:T(8,128)(2,1)S(1)} %maximum_select_fusion.8), channel_id=1, source_target_pairs={{0,2},{1,3},{2,0},{3,1},{4,6},{5,7},{6,4},{7,5},{8,10},{9,11},{10,... | collective-permute-start | bytes 3145736 | tf_op jit(solution)/shard_map/while/body/eval_jaxpr/ppermute | solution.py:41
  55.7 92.8 %collective-permute-start.2 = (bf16[512,2048]{1,0:T(8,128)(2,1)S(1)}, bf16[512,2048]{1,0:T(8,128)(2,1)}, u32[]{:S(2)}, u32[]{:S(2)}) collective-permute-start(bf16[512,2048]{1,0:T(8,128)(2,1)S(1)} %maximum_select_fusion.9), channel_id=1, source_target_pairs={{0,4},{1,5},{2,6},{3,7},{4,0},{5,1},{6,2},{7,3},{8,12},{9,13},{10,... | collective-permute-start | bytes 6291464 | tf_op jit(solution)/shard_map/while/body/eval_jaxpr/ppermute | solution.py:41
  191.3 15.6 %collective-permute-start.3 = (bf16[512,512]{1,0:T(8,128)(2,1)S(1)}, bf16[512,512]{1,0:T(8,128)(2,1)S(1)}, u32[]{:S(2)}, u32[]{:S(2)}) collective-permute-start(bf16[512,512]{1,0:T(8,128)(2,1)S(1)} %get-tuple-element.317), channel_id=1, source_target_pairs={{0,8},{8,16},{16,24},{1,9},{9,17},{17,25},{2,10},{10,18},{18,26},{... | collective-permute-start | bytes 1572872 | tf_op jit(solution)/shard_map/while/body/eval_jaxpr/ppermute | solution.py:12
  208.1 2.0 collective-permute-start
  210.4 25.4 %collective-permute-start.1 = (bf16[512,1024]{1,0:T(8,128)(2,1)S(1)}, bf16[512,1024]{1,0:T(8,128)(2,1)}, u32[]{:S(2)}, u32[]{:S(2)}) collective-permute-start(bf16[512,1024]{1,0:T(8,128)(2,1)S(1)} %maximum_select_fusion.8), channel_id=1, source_target_pairs={{0,2},{1,3},{2,0},{3,1},{4,6},{5,7},{6,4},{7,5},{8,10},{9,11},{10,... | collective-permute-start | bytes 3145736 | tf_op jit(solution)/shard_map/while/body/eval_jaxpr/ppermute | solution.py:41
  238.1 93.8 %collective-permute-start.2 = (bf16[512,2048]{1,0:T(8,128)(2,1)S(1)}, bf16[512,2048]{1,0:T(8,128)(2,1)}, u32[]{:S(2)}, u32[]{:S(2)}) collective-permute-start(bf16[512,2048]{1,0:T(8,128)(2,1)S(1)} %maximum_select_fusion.9), channel_id=1, source_target_pairs={{0,4},{1,5},{2,6},{3,7},{4,0},{5,1},{6,2},{7,3},{8,12},{9,13},{10,... | collective-permute-start | bytes 6291464 | tf_op jit(solution)/shard_map/while/body/eval_jaxpr/ppermute | solution.py:41
  374.7 15.7 %collective-permute-start.3 = (bf16[512,512]{1,0:T(8,128)(2,1)S(1)}, bf16[512,512]{1,0:T(8,128)(2,1)S(1)}, u32[]{:S(2)}, u32[]{:S(2)}) collective-permute-start(bf16[512,512]{1,0:T(8,128)(2,1)S(1)} %get-tuple-element.317), channel_id=1, source_target_pairs={{0,8},{8,16},{16,24},{1,9},{9,17},{17,25},{2,10},{10,18},{18,26},{... | collective-permute-start | bytes 1572872 | tf_op jit(solution)/shard_map/while/body/eval_jaxpr/ppermute | solution.py:12
  391.6 2.0 collective-permute-start
  393.9 25.4 %collective-permute-start.1 = (bf16[512,1024]{1,0:T(8,128)(2,1)S(1)}, bf16[512,1024]{1,0:T(8,128)(2,1)}, u32[]{:S(2)}, u32[]{:S(2)}) collective-permute-start(bf16[512,1024]{1,0:T(8,128)(2,1)S(1)} %maximum_select_fusion.8), channel_id=1, source_target_pairs={{0,2},{1,3},{2,0},{3,1},{4,6},{5,7},{6,4},{7,5},{8,10},{9,11},{10,... | collective-permute-start | bytes 3145736 | tf_op jit(solution)/shard_map/while/body/eval_jaxpr/ppermute | solution.py:41
  421.6 93.7 %collective-permute-start.2 = (bf16[512,2048]{1,0:T(8,128)(2,1)S(1)}, bf16[512,2048]{1,0:T(8,128)(2,1)}, u32[]{:S(2)}, u32[]{:S(2)}) collective-permute-start(bf16[512,2048]{1,0:T(8,128)(2,1)S(1)} %maximum_select_fusion.9), channel_id=1, source_target_pairs={{0,4},{1,5},{2,6},{3,7},{4,0},{5,1},{6,2},{7,3},{8,12},{9,13},{10,... | collective-permute-start | bytes 6291464 | tf_op jit(solution)/shard_map/while/body/eval_jaxpr/ppermute | solution.py:41
  558.1 15.7 %collective-permute-start.3 = (bf16[512,512]{1,0:T(8,128)(2,1)S(1)}, bf16[512,512]{1,0:T(8,128)(2,1)S(1)}, u32[]{:S(2)}, u32[]{:S(2)}) collective-permute-start(bf16[512,512]{1,0:T(8,128)(2,1)S(1)} %get-tuple-element.317), channel_id=1, source_target_pairs={{0,8},{8,16},{16,24},{1,9},{9,17},{17,25},{2,10},{10,18},{18,26},{... | collective-permute-start | bytes 1572872 | tf_op jit(solution)/shard_map/while/body/eval_jaxpr/ppermute | solution.py:12
  575.0 2.0 collective-permute-start
  577.3 25.4 %collective-permute-start.1 = (bf16[512,1024]{1,0:T(8,128)(2,1)S(1)}, bf16[512,1024]{1,0:T(8,128)(2,1)}, u32[]{:S(2)}, u32[]{:S(2)}) collective-permute-start(bf16[512,1024]{1,0:T(8,128)(2,1)S(1)} %maximum_select_fusion.8), channel_id=1, source_target_pairs={{0,2},{1,3},{2,0},{3,1},{4,6},{5,7},{6,4},{7,5},{8,10},{9,11},{10,... | collective-permute-start | bytes 3145736 | tf_op jit(solution)/shard_map/while/body/eval_jaxpr/ppermute | solution.py:41
  605.0 93.7 %collective-permute-start.2 = (bf16[512,2048]{1,0:T(8,128)(2,1)S(1)}, bf16[512,2048]{1,0:T(8,128)(2,1)}, u32[]{:S(2)}, u32[]{:S(2)}) collective-permute-start(bf16[512,2048]{1,0:T(8,128)(2,1)S(1)} %maximum_select_fusion.9), channel_id=1, source_target_pairs={{0,4},{1,5},{2,6},{3,7},{4,0},{5,1},{6,2},{7,3},{8,12},{9,13},{10,... | collective-permute-start | bytes 6291464 | tf_op jit(solution)/shard_map/while/body/eval_jaxpr/ppermute | solution.py:41
  741.5 15.7 %collective-permute-start.3 = (bf16[512,512]{1,0:T(8,128)(2,1)S(1)}, bf16[512,512]{1,0:T(8,128)(2,1)S(1)}, u32[]{:S(2)}, u32[]{:S(2)}) collective-permute-start(bf16[512,512]{1,0:T(8,128)(2,1)S(1)} %get-tuple-element.317), channel_id=1, source_target_pairs={{0,8},{8,16},{16,24},{1,9},{9,17},{17,25},{2,10},{10,18},{18,26},{... | collective-permute-start | bytes 1572872 | tf_op jit(solution)/shard_map/while/body/eval_jaxpr/ppermute | solution.py:12
  758.4 2.0 collective-permute-start
  760.7 25.4 %collective-permute-start.1 = (bf16[512,1024]{1,0:T(8,128)(2,1)S(1)}, bf16[512,1024]{1,0:T(8,128)(2,1)}, u32[]{:S(2)}, u32[]{:S(2)}) collective-permute-start(bf16[512,1024]{1,0:T(8,128)(2,1)S(1)} %maximum_select_fusion.8), channel_id=1, source_target_pairs={{0,2},{1,3},{2,0},{3,1},{4,6},{5,7},{6,4},{7,5},{8,10},{9,11},{10,... | collective-permute-start | bytes 3145736 | tf_op jit(solution)/shard_map/while/body/eval_jaxpr/ppermute | solution.py:41
  788.4 93.7 %collective-permute-start.2 = (bf16[512,2048]{1,0:T(8,128)(2,1)S(1)}, bf16[512,2048]{1,0:T(8,128)(2,1)}, u32[]{:S(2)}, u32[]{:S(2)}) collective-permute-start(bf16[512,2048]{1,0:T(8,128)(2,1)S(1)} %maximum_select_fusion.9), channel_id=1, source_target_pairs={{0,4},{1,5},{2,6},{3,7},{4,0},{5,1},{6,2},{7,3},{8,12},{9,13},{10,... | collective-permute-start | bytes 6291464 | tf_op jit(solution)/shard_map/while/body/eval_jaxpr/ppermute | solution.py:41
  924.9 15.7 %collective-permute-start.3 = (bf16[512,512]{1,0:T(8,128)(2,1)S(1)}, bf16[512,512]{1,0:T(8,128)(2,1)S(1)}, u32[]{:S(2)}, u32[]{:S(2)}) collective-permute-start(bf16[512,512]{1,0:T(8,128)(2,1)S(1)} %get-tuple-element.317), channel_id=1, source_target_pairs={{0,8},{8,16},{16,24},{1,9},{9,17},{17,25},{2,10},{10,18},{18,26},{... | collective-permute-start | bytes 1572872 | tf_op jit(solution)/shard_map/while/body/eval_jaxpr/ppermute | solution.py:12
  940.6 0.6 copy-start.2
